TPU v7x, 32 devices: a whole 2x2x4 slice. The times are simulated.
32 devices in a mesh: img: 2 (over x), gy: 4 (over z), gx: 4 (over y, core).
Axes of the slice: x: 2, y: 2, z: 4, core: 2. Of those that a mesh axis runs over, the one named last changes fastest.
Arguments:
- latent: float32 [4, 64, 64, 4], P('img', 'gy', 'gx'), may hold values from -6 to 6
- noise: float32 [4, 64, 64, 4], P('img', 'gy', 'gx'), may hold values from -6 to 6
- timesteps: int32 [4], P('img'), may hold values from 0 to 999, as said below
- condition: bfloat16 [4, 32, 32, 1152], P('img', 'gy', 'gx'), may hold values from -6 to 6
- embed_weight: float32 [16, 1152], replicated, may hold values from -1.5 to 1.5
- embed_bias: float32 [1152], replicated, may hold values from -3 to 3
- modulation: bfloat16 [1152, 6912], P(('gy', 'gx')), may hold values from -0.1875 to 0.1875
- modulation_bias: float32 [6912], replicated, may hold values from -2 to 2
- project_in: bfloat16 [1152, 3456], P(('gy', 'gx')), may hold values from -0.1875 to 0.1875
- project_out: bfloat16 [1152, 1152], P(('gy', 'gx')), may hold values from -1.5 to 1.5
- gate_up: bfloat16 [1152, 6144], P(('gy', 'gx')), may hold values from -0.1875 to 0.1875
- down_weight: bfloat16 [3072, 1152], P(('gy', 'gx')), may hold values from -0.109375 to 0.109375
- final_modulation: bfloat16 [1152, 2304], P(('gy', 'gx')), may hold values from -0.1875 to 0.1875
- final_offsets: float32 [2304], replicated, may hold values from -2 to 2
- final_weight: float32 [1152, 16], replicated, may hold values from -0.1875 to 0.1875
- final_bias: float32 [16], replicated, may hold values from -2 to 2
- cotangent: float32 [4, 64, 64, 4], P('img', 'gy', 'gx'), may hold values from -6 to 6
Outputs:
- prediction: float32 [4, 64, 64, 4], P('img', 'gy', 'gx')
- latent_grad: float32 [4, 64, 64, 4], P('img', 'gy', 'gx')
- condition_grad: float32 [4, 32, 32, 1152], P('img', 'gy', 'gx')
- embed_weight_grad: float32 [16, 1152], replicated
- embed_bias_grad: float32 [1152], replicated
- modulation_grad: float32 [1152, 6912], P(('gy', 'gx'))
- modulation_bias_grad: float32 [6912], replicated
- project_in_grad: float32 [1152, 3456], P(('gy', 'gx'))
- project_out_grad: float32 [1152, 1152], P(('gy', 'gx'))
- gate_up_grad: float32 [1152, 6144], P(('gy', 'gx'))
- down_weight_grad: float32 [3072, 1152], P(('gy', 'gx'))
- final_modulation_grad: float32 [1152, 2304], P(('gy', 'gx'))
- final_offsets_grad: float32 [2304], replicated
- final_weight_grad: float32 [1152, 16], replicated
- final_bias_grad: float32 [16], replicated
Inputs may be any that keep to these rules, and one draw needn't show every extreme that they name: `timesteps`: timestep index of each image, out of 1000 steps; in every draw some image has index 0 and another has index 999.
All inputs are finite; a program needn't handle non-finite values.
Results may differ from a plain program's by a relative error of at most 0.022.
Values may be sent and summed in bfloat16 or wider, within the bound.
A program may use at most 320 MiB of HBM per device.

v0:
```python
import math

import jax
import jax.numpy as jnp
from jax import lax
from jax.sharding import PartitionSpec as P

HEADS = 16
PATCH = 2


EPSILON = 1e-06


def shifted(shard, axis, by):
    size = lax.axis_size(axis)
    return lax.ppermute(shard, axis, [(i, (i + by) % size) for i in range(size)])


def modnorm(rows, scale, shift):
    normed = rows * lax.rsqrt(jnp.mean(rows * rows, axis=-1, keepdims=True) + EPSILON)
    return normed * (1.0 + scale) + shift


def gating(both):
    half = both.shape[-1] // 2
    return jax.nn.silu(both[:, :half]) * both[:, half:]


def unfold(tile):
    count, height, across, chans = tile.shape
    cut = tile.reshape(count, height // PATCH, PATCH, across // PATCH, PATCH, chans)
    return cut.transpose(0, 1, 3, 2, 4, 5).reshape(
        count * (height // PATCH) * (across // PATCH), PATCH * PATCH * chans
    )


def refold(flat, count, height, across, chans):
    cut = flat.reshape(count, height // PATCH, across // PATCH, PATCH, PATCH, chans)
    return cut.transpose(0, 1, 3, 2, 4, 5).reshape(count, height, across, chans)


def shards(
    latent,
    noise,
    timesteps,
    condition,
    embed_weight,
    embed_bias,
    modulation,
    modulation_bias,
    project_in,
    project_out,
    gate_up,
    down_weight,
    final_modulation,
    final_offsets,
    final_weight,
    final_bias,
    cotangent,
):
    highest = lax.Precision.HIGHEST
    images, height, across, chans = latent.shape
    width = condition.shape[-1]
    head = width // HEADS
    factor = 1.0 / math.sqrt(head)
    times = (timesteps.astype(jnp.float32) / 1000.0)[:, None, None, None]
    noisy = (1.0 - times) * latent + times * noise
    upper = shifted((noisy[:, -1:], cotangent[:, -1:]), "gy", 1)
    noisy = jnp.concatenate([upper[0], noisy[:, :-1]], 1)
    back_tile = jnp.concatenate([upper[1], cotangent[:, :-1]], 1)
    left = shifted((noisy[:, :, -1:], back_tile[:, :, -1:]), "gx", 1)
    noisy = jnp.concatenate([left[0], noisy[:, :, :-1]], 2)
    back_tile = jnp.concatenate([left[1], back_tile[:, :, :-1]], 2)
    gathered = (
        lax.all_gather(modulation, ("gy", "gx"), axis=0, tiled=True),
        lax.all_gather(project_in, ("gy", "gx"), axis=0, tiled=True),
        lax.all_gather(project_out, ("gy", "gx"), axis=0, tiled=True),
        lax.all_gather(gate_up, ("gy", "gx"), axis=0, tiled=True),
        lax.all_gather(down_weight, ("gy", "gx"), axis=0, tiled=True),
        lax.all_gather(final_modulation, ("gy", "gx"), axis=0, tiled=True),
    )
    modulation_all, project_in_all, project_out_all, gate_up_all, down_all, final_mod_all = gathered
    patches = unfold(noisy)
    embedded = (
        jnp.dot(patches, embed_weight, precision=highest, preferred_element_type=jnp.float32)
        + embed_bias
    )
    cond_rows = condition.reshape(-1, width).astype(jnp.float32)
    silu_cond, silu_pull = jax.vjp(jax.nn.silu, cond_rows)
    cond_act = silu_cond.astype(jnp.bfloat16)
    mod_rows = (
        jnp.dot(cond_act, modulation_all, preferred_element_type=jnp.float32) + modulation_bias
    )
    shift_a, scale_a, gate_a, shift_b, scale_b, gate_b = jnp.split(mod_rows, 6, axis=1)
    final_rows = (
        jnp.dot(cond_act, final_mod_all, preferred_element_type=jnp.float32) + final_offsets
    )
    shift_f, scale_f = jnp.split(final_rows, 2, axis=1)
    attend_in, attend_pull = jax.vjp(modnorm, embedded, scale_a, shift_a)
    attend_low = attend_in.astype(jnp.bfloat16)
    qkv = jnp.dot(attend_low, project_in_all, preferred_element_type=jnp.float32).astype(
        jnp.bfloat16
    )
    count = qkv.shape[0] // images
    queries = qkv[:, :width].reshape(images, count, HEADS, head)
    keys = qkv[:, width : 2 * width].reshape(images, count, width)
    values = qkv[:, 2 * width :].reshape(images, count, width)
    keys_all, values_all = (
        lax.all_gather(keys, ("gy", "gx"), axis=1, tiled=True),
        lax.all_gather(values, ("gy", "gx"), axis=1, tiled=True),
    )
    total_keys = keys_all.shape[1]
    keys_all = keys_all.reshape(images, total_keys, HEADS, head)
    values_all = values_all.reshape(images, total_keys, HEADS, head)
    scores = (
        jnp.einsum("bqhd,bkhd->bhqk", queries, keys_all, preferred_element_type=jnp.float32)
        * factor
    )
    top = jnp.max(scores, axis=-1, keepdims=True)
    expo = jnp.exp(scores - top)
    probs = expo / jnp.sum(expo, axis=-1, keepdims=True)
    probs_low = probs.astype(jnp.bfloat16)
    mixed = jnp.einsum("bhqk,bkhd->bqhd", probs_low, values_all, preferred_element_type=jnp.float32)
    mixed = mixed.astype(jnp.bfloat16).reshape(images * count, width)
    branch = jnp.dot(mixed, project_out_all, preferred_element_type=jnp.float32)
    h_one = embedded + gate_a * branch
    ffn_in, ffn_pull = jax.vjp(modnorm, h_one, scale_b, shift_b)
    ffn_low = ffn_in.astype(jnp.bfloat16)
    gateup = jnp.dot(ffn_low, gate_up_all, preferred_element_type=jnp.float32)
    hidden, hidden_pull = jax.vjp(gating, gateup)
    hidden_low = hidden.astype(jnp.bfloat16)
    ffn = jnp.dot(hidden_low, down_all, preferred_element_type=jnp.float32)
    h_two = h_one + gate_b * ffn
    final_in, final_pull = jax.vjp(modnorm, h_two, scale_f, shift_f)
    rows_out = (
        jnp.dot(final_in, final_weight, precision=highest, preferred_element_type=jnp.float32)
        + final_bias
    )
    pred_tile = refold(rows_out, images, height, across, chans)
    gathered = (
        lax.all_gather(modulation, ("gy", "gx"), axis=0, tiled=True),
        lax.all_gather(project_in, ("gy", "gx"), axis=0, tiled=True),
        lax.all_gather(project_out, ("gy", "gx"), axis=0, tiled=True),
        lax.all_gather(gate_up, ("gy", "gx"), axis=0, tiled=True),
        lax.all_gather(down_weight, ("gy", "gx"), axis=0, tiled=True),
        lax.all_gather(final_modulation, ("gy", "gx"), axis=0, tiled=True),
    )
    modulation_all, project_in_all, project_out_all, gate_up_all, down_all, final_mod_all = gathered
    grad_rows = unfold(back_tile)
    final_bias_grad = jnp.sum(grad_rows, axis=0)
    final_weight_grad = jnp.einsum(
        "nd,np->dp", final_in, grad_rows, precision=highest, preferred_element_type=jnp.float32
    )
    grad_final_in = jnp.einsum(
        "np,dp->nd", grad_rows, final_weight, precision=highest, preferred_element_type=jnp.float32
    )
    grad_h_two, grad_scale_f, grad_shift_f = final_pull(grad_final_in)
    grad_final = jnp.concatenate([grad_shift_f, grad_scale_f], 1)
    final_offsets_grad = jnp.sum(grad_final, axis=0)
    grad_final_low = grad_final.astype(jnp.bfloat16)
    grad_gate_b = grad_h_two * ffn
    grad_ffn = (grad_h_two * gate_b).astype(jnp.bfloat16)
    grad_hidden = jnp.einsum("nd,fd->nf", grad_ffn, down_all, preferred_element_type=jnp.float32)
    (grad_gateup,) = hidden_pull(grad_hidden)
    grad_gateup = grad_gateup.astype(jnp.bfloat16)
    grad_ffn_in = jnp.einsum(
        "nf,df->nd", grad_gateup, gate_up_all, preferred_element_type=jnp.float32
    )
    grad_h_part, grad_scale_b, grad_shift_b = ffn_pull(grad_ffn_in)
    grad_h_one = grad_h_two + grad_h_part
    final_mod_full = jnp.einsum(
        "nd,ne->de", cond_act, grad_final_low, preferred_element_type=jnp.float32
    )
    down_full = jnp.einsum("nf,nd->fd", hidden_low, grad_ffn, preferred_element_type=jnp.float32)
    gate_up_full = jnp.einsum("nd,nf->df", ffn_low, grad_gateup, preferred_element_type=jnp.float32)
    feed_shares = (
        lax.psum_scatter(
            final_mod_full.astype(jnp.bfloat16), ("gy", "gx"), scatter_dimension=0, tiled=True
        ).astype(jnp.float32),
        lax.psum_scatter(
            gate_up_full.astype(jnp.bfloat16), ("gy", "gx"), scatter_dimension=0, tiled=True
        ).astype(jnp.float32),
        lax.psum_scatter(
            down_full.astype(jnp.bfloat16), ("gy", "gx"), scatter_dimension=0, tiled=True
        ).astype(jnp.float32),
    )
    grad_gate_a = grad_h_one * branch
    grad_branch = (grad_h_one * gate_a).astype(jnp.bfloat16)
    grad_mixed = jnp.einsum(
        "ne,de->nd", grad_branch, project_out_all, preferred_element_type=jnp.float32
    )
    grad_mixed = grad_mixed.astype(jnp.bfloat16).reshape(images, count, HEADS, head)
    grad_probs = jnp.einsum(
        "bqhd,bkhd->bhqk", grad_mixed, values_all, preferred_element_type=jnp.float32
    )
    value_grad_all = jnp.einsum(
        "bhqk,bqhd->bkhd", probs_low, grad_mixed, preferred_element_type=jnp.float32
    )
    grad_scores = probs * (grad_probs - jnp.sum(grad_probs * probs, axis=-1, keepdims=True))
    grad_scores = grad_scores.astype(jnp.bfloat16)
    query_grad = (
        jnp.einsum("bhqk,bkhd->bqhd", grad_scores, keys_all, preferred_element_type=jnp.float32)
        * factor
    )
    key_grad_all = (
        jnp.einsum("bhqk,bqhd->bkhd", grad_scores, queries, preferred_element_type=jnp.float32)
        * factor
    )
    key_grad, value_grad = (
        lax.psum_scatter(
            key_grad_all.reshape(images, total_keys, width).astype(jnp.bfloat16),
            ("gy", "gx"),
            scatter_dimension=1,
            tiled=True,
        ).astype(jnp.float32),
        lax.psum_scatter(
            value_grad_all.reshape(images, total_keys, width).astype(jnp.bfloat16),
            ("gy", "gx"),
            scatter_dimension=1,
            tiled=True,
        ).astype(jnp.float32),
    )
    grad_qkv = jnp.concatenate(
        [
            query_grad.reshape(images * count, width),
            key_grad.reshape(images * count, width),
            value_grad.reshape(images * count, width),
        ],
        1,
    ).astype(jnp.bfloat16)
    grad_attend_in = jnp.einsum(
        "ne,de->nd", grad_qkv, project_in_all, preferred_element_type=jnp.float32
    )
    grad_embed_part, grad_scale_a, grad_shift_a = attend_pull(grad_attend_in)
    grad_embedded = grad_h_one + grad_embed_part
    grad_mod = jnp.concatenate(
        [grad_shift_a, grad_scale_a, grad_gate_a, grad_shift_b, grad_scale_b, grad_gate_b], 1
    )
    modulation_bias_grad = jnp.sum(grad_mod, axis=0)
    grad_mod_low = grad_mod.astype(jnp.bfloat16)
    out_full = jnp.einsum("nd,ne->de", mixed, grad_branch, preferred_element_type=jnp.float32)
    in_full = jnp.einsum("nd,ne->de", attend_low, grad_qkv, preferred_element_type=jnp.float32)
    mod_full = jnp.einsum("nd,ne->de", cond_act, grad_mod_low, preferred_element_type=jnp.float32)
    attend_shares = (
        lax.psum_scatter(
            mod_full.astype(jnp.bfloat16), ("gy", "gx"), scatter_dimension=0, tiled=True
        ).astype(jnp.float32),
        lax.psum_scatter(
            in_full.astype(jnp.bfloat16), ("gy", "gx"), scatter_dimension=0, tiled=True
        ).astype(jnp.float32),
        lax.psum_scatter(
            out_full.astype(jnp.bfloat16), ("gy", "gx"), scatter_dimension=0, tiled=True
        ).astype(jnp.float32),
    )
    grad_silu = jnp.einsum(
        "ne,de->nd", grad_mod_low, modulation_all, preferred_element_type=jnp.float32
    ) + jnp.einsum("ne,de->nd", grad_final_low, final_mod_all, preferred_element_type=jnp.float32)
    (cond_grad,) = silu_pull(grad_silu)
    condition_grad = cond_grad.reshape(condition.shape)
    embed_bias_grad = jnp.sum(grad_embedded, axis=0)
    embed_weight_grad = jnp.einsum(
        "np,nd->pd", patches, grad_embedded, precision=highest, preferred_element_type=jnp.float32
    )
    grad_patches = jnp.einsum(
        "nd,pd->np",
        grad_embedded,
        embed_weight,
        precision=highest,
        preferred_element_type=jnp.float32,
    )
    grad_tile = refold(grad_patches, images, height, across, chans)
    lower = shifted((pred_tile[:, :1], grad_tile[:, :1]), "gy", -1)
    pred_tile = jnp.concatenate([pred_tile[:, 1:], lower[0]], 1)
    grad_tile = jnp.concatenate([grad_tile[:, 1:], lower[1]], 1)
    right = shifted((pred_tile[:, :, :1], grad_tile[:, :, :1]), "gx", -1)
    prediction = jnp.concatenate([pred_tile[:, :, 1:], right[0]], 2)
    latent_grad = (1.0 - times) * jnp.concatenate([grad_tile[:, :, 1:], right[1]], 2)
    summed = (
        lax.psum(attend_shares[0].astype(jnp.bfloat16), "img").astype(jnp.float32),
        lax.psum(attend_shares[1].astype(jnp.bfloat16), "img").astype(jnp.float32),
        lax.psum(attend_shares[2].astype(jnp.bfloat16), "img").astype(jnp.float32),
        lax.psum(feed_shares[0].astype(jnp.bfloat16), "img").astype(jnp.float32),
        lax.psum(feed_shares[1].astype(jnp.bfloat16), "img").astype(jnp.float32),
        lax.psum(feed_shares[2].astype(jnp.bfloat16), "img").astype(jnp.float32),
    )
    small = lax.psum(
        (
            embed_weight_grad,
            embed_bias_grad,
            modulation_bias_grad,
            final_offsets_grad,
            final_weight_grad,
            final_bias_grad,
        ),
        ("img", "gy", "gx"),
    )
    return (
        prediction,
        latent_grad,
        condition_grad,
        small[0],
        small[1],
        summed[0],
        small[2],
        summed[1],
        summed[2],
        summed[4],
        summed[5],
        summed[3],
        small[3],
        small[4],
        small[5],
    )


def solution(mesh):
    in_specs = (
        P("img", "gy", "gx", None),
        P("img", "gy", "gx", None),
        P("img"),
        P("img", "gy", "gx", None),
        P(),
        P(),
        P(("gy", "gx"), None),
        P(),
        P(("gy", "gx"), None),
        P(("gy", "gx"), None),
        P(("gy", "gx"), None),
        P(("gy", "gx"), None),
        P(("gy", "gx"), None),
        P(),
        P(),
        P(),
        P("img", "gy", "gx", None),
    )
    out_specs = (
        P("img", "gy", "gx", None),
        P("img", "gy", "gx", None),
        P("img", "gy", "gx", None),
        P(),
        P(),
        P(("gy", "gx"), None),
        P(),
        P(("gy", "gx"), None),
        P(("gy", "gx"), None),
        P(("gy", "gx"), None),
        P(("gy", "gx"), None),
        P(("gy", "gx"), None),
        P(),
        P(),
        P(),
    )
    return jax.shard_map(shards, mesh=mesh, in_specs=in_specs, out_specs=out_specs, check_vma=False)
```

profile of v0, /device:TPU:1, one launch (start us, length us, event | category | flops | bytes accessed | tf_op | source)
XLA Modules:
  0.0 1699.8 jit_solution(5521557801745383364)
XLA Ops:
  22.5 111.8 %all-gather.9.cloned.1.call-done = bf16[1152,6912]{1,0:T(8,128)(2,1)} async-done(((bf16[72,6912]{1,0:T(8,128)(2,1)}), bf16[1152,6912]{1,0:T(8,128)(2,1)}) %all-gather.9.cloned.1.call-update) | async-done | bytes 15925264 | tf_op jit(solution)/shard_map/all_gather | solution.py:76
  134.3 8.1 convolution_add_fusion
  144.3 62.5 %all-gather.11.cloned.1.call-done = bf16[1152,3456]{1,0:T(8,128)(2,1)} async-done(((bf16[72,3456]{1,0:T(8,128)(2,1)}), bf16[1152,3456]{1,0:T(8,128)(2,1)}) %all-gather.11.cloned.1.call-update) | async-done | bytes 7962640 | tf_op jit(solution)/shard_map/all_gather | solution.py:77
  223.7 40.3 %all-gather.23.cloned.1.call-done = bf16[1152,2304]{1,0:T(8,128)(2,1)} async-done(((bf16[72,2304]{1,0:T(8,128)(2,1)}), bf16[1152,2304]{1,0:T(8,128)(2,1)}) %all-gather.23.cloned.1.call-update) | async-done | bytes 5308432 | tf_op jit(solution)/shard_map/all_gather | solution.py:81
  270.2 48.5 %all-gather.15.cloned.1.call-done = bf16[2,1024,1152]{2,1,0:T(8,128)(2,1)} async-done(((bf16[2,64,1152]{2,1,0:T(8,128)(2,1)}), bf16[2,1024,1152]{2,1,0:T(8,128)(2,1)}) %all-gather.15.cloned.1.call-update) | async-done | bytes 4718608 | tf_op jit(solution)/shard_map/all_gather | solution.py:110
  325.4 48.0 %all-gather.13.cloned.1.call-done = bf16[2,1024,1152]{2,1,0:T(8,128)(2,1)} async-done(((bf16[2,64,1152]{2,1,0:T(8,128)(2,1)}), bf16[2,1024,1152]{2,1,0:T(8,128)(2,1)}) %all-gather.13.cloned.1.call-update) | async-done | bytes 4718608 | tf_op jit(solution)/shard_map/all_gather | solution.py:111
  399.3 18.1 %all-gather.17.cloned.1.call-done = bf16[1152,1152]{1,0:T(8,128)(2,1)} async-done(((bf16[72,1152]{1,0:T(8,128)(2,1)}), bf16[1152,1152]{1,0:T(8,128)(2,1)}) %all-gather.17.cloned.1.call-update) | async-done | bytes 2654224 | tf_op jit(solution)/shard_map/all_gather | solution.py:78
  422.1 106.9 %all-gather.19.cloned.1.call-done = bf16[1152,6144]{1,0:T(8,128)(2,1)} async-done(((bf16[72,6144]{1,0:T(8,128)(2,1)}), bf16[1152,6144]{1,0:T(8,128)(2,1)}) %all-gather.19.cloned.1.call-update) | async-done | bytes 14155792 | tf_op jit(solution)/shard_map/all_gather | solution.py:79
  538.5 57.6 %all-gather.21.cloned.1.call-done = bf16[3072,1152]{1,0:T(8,128)(2,1)} async-done(((bf16[192,1152]{1,0:T(8,128)(2,1)}), bf16[3072,1152]{1,0:T(8,128)(2,1)}) %all-gather.21.cloned.1.call-update) | async-done | bytes 7077904 | tf_op jit(solution)/shard_map/all_gather | solution.py:80
  609.0 11.6 multiply_reduce_fusion.3
  686.1 27.2 %reduce-scatter.15.cloned.1.call-done = bf16[2,64,1152]{2,1,0:T(8,128)(2,1)} async-done(((bf16[2,1024,1152]{2,1,0:T(8,128)(2,1)}), bf16[2,64,1152]{2,1,0:T(8,128)(2,1)}) %reduce-scatter.15.cloned.1.call-update) | async-done | bytes 294928 | tf_op jit(solution)/shard_map/reduce_scatter | solution.py:217
  713.3 78.9 %reduce-scatter.13.cloned.1.call-done = bf16[2,64,1152]{2,1,0:T(8,128)(2,1)} async-done(((bf16[2,1024,1152]{2,1,0:T(8,128)(2,1)}), bf16[2,64,1152]{2,1,0:T(8,128)(2,1)}) %reduce-scatter.13.cloned.1.call-update) | async-done | bytes 294928 | tf_op jit(solution)/shard_map/reduce_scatter | solution.py:211
  799.6 9.1 convolution_convert_fusion.1
  823.0 10.2 convolution_convert_fusion
  833.4 25.0 %reduce-scatter.27.cloned.1.call-done = bf16[72,1152]{1,0:T(8,128)(2,1)} async-done(((bf16[1152,1152]{1,0:T(8,128)(2,1)}), bf16[72,1152]{1,0:T(8,128)(2,1)}) %reduce-scatter.27.cloned.1.call-update) | async-done | bytes 165904
  858.4 83.0 %reduce-scatter.23.cloned.1.call-done = bf16[72,2304]{1,0:T(8,128)(2,1)} async-done(((bf16[1152,2304]{1,0:T(8,128)(2,1)}), bf16[72,2304]{1,0:T(8,128)(2,1)}) %reduce-scatter.23.cloned.1.call-update) | async-done | bytes 331792 | tf_op jit(solution)/shard_map/reduce_scatter | solution.py:178
  941.4 94.9 %reduce-scatter.21.cloned.1.call-done = bf16[192,1152]{1,0:T(8,128)(2,1)} async-done(((bf16[3072,1152]{1,0:T(8,128)(2,1)}), bf16[192,1152]{1,0:T(8,128)(2,1)}) %reduce-scatter.21.cloned.1.call-update) | async-done | bytes 442384 | tf_op jit(solution)/shard_map/reduce_scatter | solution.py:184
  1036.3 104.5 %reduce-scatter.25.cloned.1.call-done = bf16[72,3456]{1,0:T(8,128)(2,1)} async-done(((bf16[1152,3456]{1,0:T(8,128)(2,1)}), bf16[72,3456]{1,0:T(8,128)(2,1)}) %reduce-scatter.25.cloned.1.call-update) | async-done | bytes 497680
  1140.8 149.2 %reduce-scatter.19.cloned.1.call-done = bf16[72,6144]{1,0:T(8,128)(2,1)} async-done(((bf16[1152,6144]{1,0:T(8,128)(2,1)}), bf16[72,6144]{1,0:T(8,128)(2,1)}) %reduce-scatter.19.cloned.1.call-update) | async-done | bytes 884752 | tf_op jit(solution)/shard_map/reduce_scatter | solution.py:181
  1290.0 176.5 %reduce-scatter.17.cloned.1.call-done = bf16[72,6912]{1,0:T(8,128)(2,1)} async-done(((bf16[1152,6912]{1,0:T(8,128)(2,1)}), bf16[72,6912]{1,0:T(8,128)(2,1)}) %reduce-scatter.17.cloned.1.call-update) | async-done | bytes 995344 | tf_op jit(solution)/shard_map/reduce_scatter | solution.py:246
  1484.0 11.8 fusion.22
  1501.1 38.2 %all-reduce.4 = (f32[1152]{0:T(1024)}, f32[6912]{0:T(1024)}, f32[2304]{0:T(1024)}, f32[16]{0:T(128)}) all-reduce(f32[1152]{0:T(1024)S(1)} %get-tuple-element.59, f32[6912]{0:T(1024)S(1)} %reduce_sum.131, f32[2304]{0:T(1024)S(1)} %fusion.19, f32[16]{0:T(128)S(1)} %reduce_sum.134), channel_id=1, replica_groups=mesh['img'=2,'gy'=4,'gx'=4] {'img','gy','gx'}, use_global_device_ids=true, to_apply=%region_13.14 | all-reduce | flops 10384 | bytes 83072 | tf_op jit(solution)/shard_map/psum | solution.py:287
  1545.4 14.6 all-reduce.12.cloned.1.call-done
  1570.6 118.9 %all-reduce.10.cloned.1.call-done = (f32[16,1152]{1,0:T(8,128)}, f32[1152,16]{0,1:T(8,128)}) async-done(((f32[16,1152]{1,0:T(8,128)}, f32[1152,16]{0,1:T(8,128)}), (f32[16,1152]{1,0:T(8,128)}, f32[1152,16]{0,1:T(8,128)})) %all-reduce.10.cloned.1.call-update) | async-done | bytes 147472 | tf_op jit(solution)/shard_map/psum | solution.py:287
  (243 shorter events, 229.0 us)
Async XLA Ops:
  7.2 127.1 %all-gather.9.cloned.1.call-start = ((), (), s32[]{:S(2)}) async-start(), calls=%async_computation.8 | async-start | bytes 16920576 | tf_op jit(solution)/shard_map/all_gather | solution.py:76
  8.0 198.9 %all-gather.11.cloned.1.call-start = ((), (), s32[]{:S(2)}) async-start(), calls=%async_computation.9 | async-start | bytes 8460288 | tf_op jit(solution)/shard_map/all_gather | solution.py:77
  8.7 255.3 %all-gather.23.cloned.1.call-start = ((), (), s32[]{:S(2)}) async-start(), calls=%async_computation.15 | async-start | bytes 5640192 | tf_op jit(solution)/shard_map/all_gather | solution.py:81
  9.4 309.3 %all-gather.15.cloned.1.call-start = ((), (), s32[]{:S(2)}) async-start(), calls=%async_computation.11 | async-start | bytes 5013504 | tf_op jit(solution)/shard_map/all_gather | solution.py:110
  11.1 5.2 collective-permute-start
  16.4 4.3 collective-permute-start.1
  212.5 160.9 %all-gather.13.cloned.1.call-start = ((), (), s32[]{:S(2)}) async-start(), calls=%async_computation.10 | async-start | bytes 5013504 | tf_op jit(solution)/shard_map/all_gather | solution.py:111
  213.1 204.3 %all-gather.17.cloned.1.call-start = ((), (), s32[]{:S(2)}) async-start(), calls=%async_computation.12 | async-start | bytes 2820096 | tf_op jit(solution)/shard_map/all_gather | solution.py:78
  213.7 315.3 %all-gather.19.cloned.1.call-start = ((), (), s32[]{:S(2)}) async-start(), calls=%async_computation.13 | async-start | bytes 15040512 | tf_op jit(solution)/shard_map/all_gather | solution.py:79
  214.4 381.7 %all-gather.21.cloned.1.call-start = ((), (), s32[]{:S(2)}) async-start(), calls=%async_computation.14 | async-start | bytes 7520256 | tf_op jit(solution)/shard_map/all_gather | solution.py:80
  215.2 498.1 %reduce-scatter.15.cloned.1.call-start = ((), (), s32[]{:S(2)}) async-start(), calls=%async_computation.17 | async-start | bytes 5013504 | tf_op jit(solution)/shard_map/reduce_scatter | solution.py:217
  215.2 4.5 collective-permute-start.4
  640.5 151.6 %reduce-scatter.13.cloned.1.call-start = ((), (), s32[]{:S(2)}) async-start(), calls=%async_computation.16 | async-start | bytes 5013504 | tf_op jit(solution)/shard_map/reduce_scatter | solution.py:211
  662.7 195.6 %reduce-scatter.27.cloned.1.call-start = ((), (), s32[]{:S(2)}) async-start(), calls=%async_computation.23 | async-start | bytes 2820096
  667.1 274.3 %reduce-scatter.23.cloned.1.call-start = ((), (), s32[]{:S(2)}) async-start(), calls=%async_computation.21 | async-start | bytes 5640192 | tf_op jit(solution)/shard_map/reduce_scatter | solution.py:178
  672.2 364.1 %reduce-scatter.21.cloned.1.call-start = ((), (), s32[]{:S(2)}) async-start(), calls=%async_computation.20 | async-start | bytes 7520256 | tf_op jit(solution)/shard_map/reduce_scatter | solution.py:184
  678.1 462.7 %reduce-scatter.25.cloned.1.call-start = ((), (), s32[]{:S(2)}) async-start(), calls=%async_computation.22 | async-start | bytes 8460288
  798.6 491.3 %reduce-scatter.19.cloned.1.call-start = ((), (), s32[]{:S(2)}) async-start(), calls=%async_computation.19 | async-start | bytes 15040512 | tf_op jit(solution)/shard_map/reduce_scatter | solution.py:181
  808.7 657.8 %reduce-scatter.17.cloned.1.call-start = ((), (), s32[]{:S(2)}) async-start(), calls=%async_computation.18 | async-start | bytes 16920576 | tf_op jit(solution)/shard_map/reduce_scatter | solution.py:246
  833.3 726.7 %all-reduce.12.cloned.1.call-start = ((), (), s32[]{:S(2)}) async-start(), calls=%async_computation.25 | async-start | bytes 6635520 | tf_op jit(solution)/shard_map/psum | solution.py:280
  1466.5 223.0 %all-reduce.10.cloned.1.call-start = ((), (), s32[]{:S(2)}) async-start(), calls=%async_computation.24 | async-start | bytes 294912 | tf_op jit(solution)/shard_map/psum | solution.py:287
  1470.7 4.8 collective-permute-start.3
  1479.7 59.9 %collective-permute-start.6 = (f32[2,1,16,4]{3,2,1,0:T(8,128)S(1)}, f32[2,1,16,4]{3,2,1,0:T(8,128)S(1)}, u32[]{:S(2)}, u32[]{:S(2)}) collective-permute-start(f32[2,1,16,4]{3,2,1,0:T(8,128)S(1)} %slice.100), channel_id=1, source_target_pairs={{0,12},{4,0},{8,4},{12,8},{1,13},{5,1},{9,5},{13,9},{2,14},{6,2},{... | collective-permute-start | bytes 1544 | tf_op jit(solution)/shard_map/ppermute | solution.py:17
  1539.7 4.9 collective-permute-start.7
  (47 other events, 3886.0 us)
Sparse Core Ops, SparseCore 0:
  10.2 124.0 all-gather.8
  136.5 70.3 all-gather.10
  209.1 54.8 all-gather.22
  266.7 51.9 all-gather.14
  321.4 51.9 all-gather.12
  375.4 41.9 all-gather.16
  419.7 109.2 all-gather.18
  531.3 64.7 all-gather.20
  640.7 72.5 reduce-scatter.14
  717.5 74.6 reduce-scatter.12
  796.1 62.2 reduce-scatter.26
  862.8 78.5 reduce-scatter.22
  945.9 90.2 reduce-scatter.20
  1040.2 100.5 reduce-scatter.24
  1145.3 144.5 reduce-scatter.18
  1294.5 171.8 reduce-scatter.16
  1469.1 90.8 all-reduce.11
  1566.6 122.8 all-reduce.9
where the time goes:
time: 1710 us; the launch traced here: 1700 us
  waiting for transfers between devices  1390 us (81%)
  matrix products  151 us (9%)
  local copies, waits for them, and re-layouts  53.3 us (3%)
  other arithmetic  40 us (2%)
  blocking collectives  38.2 us (2%)
    reduce_scatter x1, waiting for transfers between devices, shards(): lax.psum_scatter(mod_full.astype(jnp.bfloat16), ('gy', 'gx'), scatter_dim...  176 us
    reduce_scatter x1, waiting for transfers between devices, shards(): lax.psum_scatter(gate_up_full.astype(jnp.bfloat16), ('gy', 'gx'), scatter...  149 us
    unnamed x20, waiting for transfers between devices  134 us
    psum x1, waiting for transfers between devices, shards(): lax.psum((embed_weight_grad, embed_bias_grad, modulation_bias_grad, final...  119 us
    all_gather x1, waiting for transfers between devices, shards(): lax.all_gather(modulation, ('gy', 'gx'), axis=0, tiled=True)  112 us
    all_gather x1, waiting for transfers between devices, shards(): lax.all_gather(gate_up, ('gy', 'gx'), axis=0, tiled=True)  107 us
    reduce_scatter x1, waiting for transfers between devices, shards(): lax.psum_scatter(down_full.astype(jnp.bfloat16), ('gy', 'gx'), scatter_di...  94.9 us
    reduce_scatter x1, waiting for transfers between devices, shards(): lax.psum_scatter(final_mod_full.astype(jnp.bfloat16), ('gy', 'gx'), scatt...  83 us
  transfers between devices with their start and end apart: 26, of which 25 were waited for; matrix products, arithmetic and copies ran while one was open for 11% of the time, Pallas kernels for 0%

commit v1 on v0

v1 whole, which is shorter than its diff:
```python
import functools
import math

import jax
import jax.numpy as jnp
from jax import lax
from jax.experimental import pallas as pl
from jax.experimental.pallas import tpu as pltpu
from jax.sharding import Mesh
from jax.sharding import PartitionSpec as P

HEADS = 16
PATCH = 2
EPSILON = 1e-06
MESH = pl.DeviceIdType.MESH
BF16 = jnp.bfloat16
F32 = jnp.float32
RANKS = 8


def rank_of():
    return lax.axis_index("l") * 4 + lax.axis_index("gx")


def in_group(rank):
    return {"l": rank // 4, "gx": lax.rem(rank, 4)}


def in_plane(place):
    return {"h": place // 8, "l": lax.rem(place // 4, 2), "gx": lax.rem(place, 4)}


CHIPS = 4


class Place:
    def __init__(self):
        self.l = lax.axis_index("l")
        across = lax.axis_index("gx")
        self.y = lax.div(across, 2)
        self.core = lax.rem(across, 2)

    def chip(self, k):
        dl, dy = lax.div(k, 2), lax.rem(k, 2)
        return self.l + dl - 2 * self.l * dl, self.y + dy - 2 * self.y * dy

    def rows(self, k):
        row, col = self.chip(k)
        return pl.ds((row * 2 + col) * 2, 2)

    def slot(self, k, flip):
        row, col = self.chip(k)
        return (row * 2 + col) * 2 + (1 - self.core if flip else self.core)

    def device(self, k, flip):
        row, col = self.chip(k)
        return {"l": row, "gx": col * 2 + (1 - self.core if flip else self.core)}

    def greet(self, everyone, across=False):
        barrier = pltpu.get_barrier_semaphore()
        peers = [(0, True)] + [(k, False) for k in range(1, CHIPS)]
        if everyone:
            peers += [(k, True) for k in range(1, CHIPS)]
        for k, flip in peers:
            pl.semaphore_signal(barrier, inc=1, device_id=self.device(k, flip), device_id_type=MESH)
        if across:
            other = {"x": 1 - lax.axis_index("x")}
            pl.semaphore_signal(barrier, inc=1, device_id=other, device_id_type=MESH)
        pl.semaphore_wait(barrier, len(peers) + across)


def sent(src, dst, sems, kind, k, device):
    return pltpu.make_async_remote_copy(
        src_ref=src, dst_ref=dst, send_sem=sems.at[kind, k], recv_sem=sems.at[kind + 1, k],
        device_id=device, device_id_type=MESH,
    )


class Gather:
    def __init__(self, place, buf, sems):
        self.place, self.buf, self.sems = place, buf, sems

    def link(self, k):
        mine = self.buf.at[self.place.slot(0, False)]
        return sent(mine, mine, self.sems, 0, k, self.place.device(k, False))

    def pair(self, k):
        block = self.buf.at[self.place.slot(k, False)]
        return sent(block, block, self.sems, 2, k, self.place.device(0, True))

    def start(self):
        for k in range(1, CHIPS):
            self.link(k).start()
        self.pair(0).start()

    def arrive(self, k):
        def forward(n):
            self.link(n).wait_recv()
            self.pair(n).start()

        @pl.when(k == 1)
        def _():
            forward(1)
            forward(2)

        @pl.when(k == 3)
        def _():
            forward(3)

        self.pair(k).wait_recv()

    def finish(self):
        for k in range(CHIPS):
            if k:
                self.link(k).wait_send()
            self.pair(k).wait_send()


class Scatter:
    def __init__(self, place, refs, sems):
        self.place, self.sems = place, sems
        self.both, self.got, self.out, self.land, self.total = refs

    def pair(self, k):
        return sent(
            self.both.at[k, 1 - self.place.core], self.got.at[k], self.sems, 4, k,
            self.place.device(0, True),
        )

    def link(self, k):
        return sent(self.out.at[k], self.land.at[k], self.sems, 6, k, self.place.device(k, False))

    def put(self, k, part):
        self.both[k] = part.astype(BF16).reshape(self.both.shape[1:])
        self.pair(k).start()

    def pass_on(self, k):
        self.pair(k).wait_recv()
        added = self.both[k, self.place.core].astype(F32) + self.got[k].astype(F32)

        @pl.when(k == 0)
        def _():
            self.total[...] = added

        @pl.when(k > 0)
        def _():
            self.out[k] = added.astype(BF16)
            self.link(k).start()

    def finish(self):
        for k in range(1, CHIPS):
            self.link(k).wait_recv()
            self.total[...] += self.land[k].astype(F32)
        for k in range(CHIPS):
            if k:
                self.link(k).wait_send()
            self.pair(k).wait_send()


def scatter_scratch(rows, width):
    return [
        pltpu.VMEM((CHIPS, 2, rows, width), BF16),
        pltpu.VMEM((CHIPS, rows, width), BF16),
        pltpu.VMEM((CHIPS, rows, width), BF16),
        pltpu.VMEM((CHIPS, rows, width), BF16),
    ]


def chips(body):
    lax.fori_loop(0, CHIPS, lambda k, carry: (body(k), carry)[1], 0)


def mat(value):
    return value.reshape(-1, value.shape[-1])


def product(left, right, contract):
    return lax.dot_general(
        left, right, ((contract[:1], contract[1:]), ((), ())), preferred_element_type=F32
    )


def grads_into(out_ref, left_ref, right_ref, pick=None, tile=128):
    right = mat(right_ref[...])

    def body(i, carry):
        cols = pl.ds(pl.multiple_of(i * tile, tile), tile)
        part = product(mat(left_ref[:, :, cols]), right, (0, 0)).astype(out_ref.dtype)
        if pick is not None:
            part = product(part, pick, (1, 0)).astype(out_ref.dtype)
        out_ref[cols, :] = part
        return carry

    lax.fori_loop(0, left_ref.shape[-1] // tile, body, 0)


def attend_kernel(
    factor, head, own, in_narrow, out_weight, total, attend_all, qkv, mixed, in_weight,
    both, got, out, land, sems,
):
    place = Place()
    place.greet(False)
    attend_all[place.slot(0, False)] = own[...]
    gather = Gather(place, attend_all, sems)
    gather.start()
    lanes = mixed.shape[-1] // 2
    pick = selection(6 * lanes, head, lanes)
    in_weight[...] = product(in_narrow[...], pick, (1, 1)).astype(BF16)

    def first(k):
        gather.arrive(k)
        rows = place.rows(k)
        part = product(mat(attend_all[rows]), in_weight[...], (1, 0)).astype(BF16)
        qkv[rows] = part.reshape(2, -1, part.shape[-1])

    chips(first)
    gather.finish()
    scatter = Scatter(place, (both, got, out, land, total), sems)

    def second(step):
        k = CHIPS - 1 - step
        rows = place.rows(k)
        for head in range(2):
            span = [pl.ds((part * 2 + head) * lanes, lanes) for part in range(3)]
            queries = mat(qkv[rows, :, span[0]])
            keys, values = mat(qkv[:, :, span[1]]), mat(qkv[:, :, span[2]])
            scores = product(keys, queries, (1, 1)) * factor
            expo = jnp.exp(scores - jnp.max(scores, axis=0, keepdims=True))
            probs = expo * (1.0 / jnp.sum(expo, axis=0, keepdims=True))
            gained = product(probs.astype(BF16), values, (0, 0)).astype(BF16)
            mixed[rows, :, span[0]] = gained.reshape(2, -1, lanes)
        scatter.put(k, product(mat(mixed[rows]), out_weight[...], (1, 0)))

        @pl.when(step > 0)
        def _():
            scatter.pass_on(k + 1)

    chips(second)
    scatter.pass_on(0)
    scatter.finish()


def feed_kernel(own, gate_weight, down_weight, total, ffn_all, gateup, both, got, out, land, sems):
    place = Place()
    place.greet(False)
    ffn_all[place.slot(0, False)] = own[...]
    gather = Gather(place, ffn_all, sems)
    gather.start()
    scatter = Scatter(place, (both, got, out, land, total), sems)
    share = down_weight.shape[0]

    def body(k):
        gather.arrive(k)
        rows = place.rows(k)
        part = product(mat(ffn_all[rows]), gate_weight[...], (1, 0))
        gateup[rows] = part.reshape(2, -1, 2 * share)
        gate, up = part[:, :share], part[:, share:]
        hidden = (gate * sigma(gate) * up).astype(BF16)
        scatter.put(k, product(hidden, down_weight[...], (1, 0)))

        @pl.when(k > 0)
        def _():
            scatter.pass_on(k - 1)

    chips(body)
    scatter.pass_on(CHIPS - 1)
    gather.finish()
    scatter.finish()


def feed_back_kernel(
    own, gate_weight, down_weight, gateup, ffn_all, total, gate_grad, down_grad,
    grad_all, grad_gateup, hidden_all, both, got, out, land, sems,
):
    place = Place()
    place.greet(False)
    grad_all[place.slot(0, False)] = own[...]
    gather = Gather(place, grad_all, sems)
    gather.start()
    scatter = Scatter(place, (both, got, out, land, total), sems)
    share = down_weight.shape[0]

    def body(k):
        gather.arrive(k)
        rows = place.rows(k)
        grad_hidden = product(mat(grad_all[rows]), down_weight[...], (1, 1))
        part = mat(gateup[rows])
        gate, up = part[:, :share], part[:, share:]
        gate_sigma = sigma(gate)
        silu = gate * gate_sigma
        hidden_all[rows] = (silu * up).astype(BF16).reshape(2, -1, share)
        grad_gate = grad_hidden * up * gate_sigma * (1.0 + gate * (1.0 - gate_sigma))
        both_grads = jnp.concatenate([grad_gate, grad_hidden * silu], 1).astype(BF16)
        grad_gateup[rows] = both_grads.reshape(2, -1, 2 * share)
        scatter.put(k, product(both_grads, gate_weight[...], (1, 1)))

        @pl.when(k > 0)
        def _():
            scatter.pass_on(k - 1)

    chips(body)
    scatter.pass_on(CHIPS - 1)
    gather.finish()
    grads_into(down_grad, hidden_all, grad_all)
    grads_into(gate_grad, ffn_all, grad_gateup)
    scatter.finish()


def attend_back_kernel(
    factor, head_size, own, in_weight, out_weight, attend_all, qkv, mixed, gate_grad, down_grad,
    total, in_grad, out_grad, gate_land, down_land,
    grad_all, grad_mixed, grad_qkv, key_sum, value_sum, both, got, out, land, cross, sems,
):
    place = Place()
    place.greet(False, True)
    crossings = (
        Crossing(gate_grad, gate_land, cross, 0, gate_land.shape[1]),
        Crossing(down_grad, down_land, cross, 1, down_land.shape[0], False),
    )
    for crossing in crossings:
        crossing.start()
    grad_all[place.slot(0, False)] = own[...]
    gather = Gather(place, grad_all, sems)
    gather.start()
    lanes = mixed.shape[-1] // 2
    key_sum[...] = jnp.zeros_like(key_sum)
    value_sum[...] = jnp.zeros_like(value_sum)

    def first(k):
        gather.arrive(k)
        rows = place.rows(k)
        part = product(mat(grad_all[rows]), out_weight[...], (1, 1)).astype(BF16)
        grad_mixed[rows] = part.reshape(2, -1, 2 * lanes)
        for head in range(2):
            span = [pl.ds((part * 2 + head) * lanes, lanes) for part in range(3)]
            queries, grads = mat(qkv[rows, :, span[0]]), mat(grad_mixed[rows, :, span[0]])
            keys, values = mat(qkv[:, :, span[1]]), mat(qkv[:, :, span[2]])
            scores = product(keys, queries, (1, 1)) * factor
            expo = jnp.exp(scores - jnp.max(scores, axis=0, keepdims=True))
            probs = expo * (1.0 / jnp.sum(expo, axis=0, keepdims=True))
            value_sum[head] += product(probs.astype(BF16), grads, (1, 0))
            grad_probs = product(values, grads, (1, 1))
            middle = jnp.sum(grad_probs * probs, axis=0, keepdims=True)
            grad_scores = (probs * (grad_probs - middle)).astype(BF16)
            key_sum[head] += product(grad_scores, queries, (1, 0))
            back = (product(grad_scores, keys, (0, 0)) * factor).astype(BF16)
            grad_qkv[rows, :, span[0]] = back.reshape(2, -1, lanes)

    chips(first)
    gather.finish()
    for head in range(2):
        span = [pl.ds((part * 2 + head) * lanes, lanes) for part in range(3)]
        high = grad_qkv.shape[1]
        keys = (key_sum[head] * factor).astype(BF16)
        grad_qkv[:, :, span[1]] = keys.reshape(-1, high, lanes)
        grad_qkv[:, :, span[2]] = value_sum[head].astype(BF16).reshape(-1, high, lanes)
    scatter = Scatter(place, (both, got, out, land, total), sems)

    def second(step):
        k = CHIPS - 1 - step
        scatter.put(k, product(mat(grad_qkv[place.rows(k)]), in_weight[...], (1, 1)))

        @pl.when(step > 0)
        def _():
            scatter.pass_on(k + 1)

    chips(second)
    scatter.pass_on(0)
    grads_into(out_grad, mixed, grad_all)
    pick = selection(6 * lanes, head_size, lanes)
    grads_into(in_grad, attend_all, grad_qkv, pick)
    scatter.finish()
    for crossing in crossings:
        crossing.wait()


def mod_back_kernel(
    own, weight, cond_all, in_grad, out_grad, total, mod_grad, in_land, out_land,
    grad_all, both, got, out, land, cross, sems,
):
    place = Place()
    place.greet(True, True)
    crossings = (
        Crossing(in_grad, in_land, cross, 0, in_land.shape[1]),
        Crossing(out_grad, out_land, cross, 1, out_land.shape[0], False),
    )
    for crossing in crossings:
        crossing.start()
    me = place.slot(0, False)

    def give(k, flip):
        return sent(
            own.at[place.slot(k, flip)], grad_all.at[me], sems, 2 if flip else 0, k,
            place.device(k, flip),
        )

    for k in range(1, CHIPS):
        for flip in (False, True):
            give(k, flip).start()
    give(0, True).start()
    grad_all[me] = own[me]
    scatter = Scatter(place, (both, got, out, land, total), sems)

    def body(k):
        give(k, True).wait_recv()

        @pl.when(k > 0)
        def _():
            give(k, False).wait_recv()

        scatter.put(k, product(mat(grad_all[place.rows(k)]), weight[...], (1, 1)))

        @pl.when(k > 0)
        def _():
            scatter.pass_on(k - 1)

    chips(body)
    scatter.pass_on(CHIPS - 1)
    grads_into(mod_grad, cond_all, grad_all)
    for k in range(CHIPS):
        give(k, True).wait_send()
        if k:
            give(k, False).wait_send()
    scatter.finish()
    for crossing in crossings:
        crossing.wait()


def segment(kernel, number, operands, outs, scratch, scatters, crosses=False):
    work = [pltpu.VMEM(shape, kind) for shape, kind in scratch]
    work += scatter_scratch(*scatters)
    if crosses:
        work.append(pltpu.SemaphoreType.DMA((2, 2, RANKS)))
    name = getattr(kernel, "func", kernel).__name__
    return pl.pallas_call(
        kernel,
        out_shape=tuple(jax.ShapeDtypeStruct(shape, kind) for shape, kind in outs),
        in_specs=[pl.BlockSpec(memory_space=pltpu.VMEM)] * len(operands),
        out_specs=tuple(pl.BlockSpec(memory_space=pltpu.VMEM) for _ in outs),
        scratch_shapes=[*work, pltpu.SemaphoreType.DMA((8, CHIPS))],
        compiler_params=pltpu.CompilerParams(
            collective_id=number, has_side_effects=True, vmem_limit_bytes=60 << 20
        ),
        name=name,
    )(*operands)


PLACES = 2 * RANKS


def copied(src, dst, send_sem, recv_sem, device):
    return pltpu.make_async_remote_copy(
        src_ref=src, dst_ref=dst, send_sem=send_sem, recv_sem=recv_sem,
        device_id=device, device_id_type=MESH,
    )


def greet_plane(me, half):
    barrier = pltpu.get_barrier_semaphore()
    for step in range(1, PLACES):
        pl.semaphore_signal(
            barrier, inc=1, device_id=in_plane(lax.rem(me + step, PLACES)), device_id_type=MESH
        )
    pl.semaphore_signal(barrier, inc=1, device_id={"x": 1 - half}, device_id_type=MESH)
    pl.semaphore_wait(barrier, PLACES)


def loop(count, body):
    lax.fori_loop(0, count, lambda i, carry: (body(i), carry)[1], 0)


def start_kernel(
    modulation, final_modulation, gate_up, in_cols, project_out, down, condition,
    mods, cond_all, cond_own, mod_w, gate_w, in_w, out_w, down_w,
    stage, sems, w_send, w_recv, xs_send, xs_recv, r_send, r_recv, own_sem, c_sem,
):
    place = Place()
    half, group, rank = lax.axis_index("x"), lax.axis_index("h"), rank_of()
    me = group * RANKS + rank
    high, width = project_out.shape
    share = gate_w.shape[1] // 2
    blocks = modulation.shape[1] // width
    across = {"x": 1 - half}
    mine = lax.div(me, 2)
    sends = lax.rem(me, 2) == half
    pad = out_w.shape[1] - high
    out_w[:, pl.ds(high, pad)] = jnp.zeros((2, pad, width), BF16)
    greet_plane(me, half)

    partner = copied(
        condition.at[1 - group], cond_own.at[group], c_sem.at[0], c_sem.at[1], {"h": 1 - group}
    )
    partner.start()

    def rows_of(number):
        return pl.ds(pl.multiple_of(number * high, 8), high)

    def lanes_of(number, count):
        return pl.ds(pl.multiple_of(number * count, 128), count)

    def source_of(kind, target, then):
        if kind == 0:

            @pl.when(target < blocks)
            def _():
                then(modulation.at[:, lanes_of(target, width)])

            @pl.when(target >= blocks)
            def _():
                then(final_modulation.at[:, lanes_of(target - blocks, width)])
        elif kind == 3:
            then(in_cols.at[target])
        else:
            then(gate_up.at[:, lanes_of((kind - 1) * RANKS + target, share)])

    def landing(kind, number):
        if kind == 0:
            return mod_w.at[rows_of(number)]
        if kind == 3:
            return in_w.at[rows_of(number)]
        return gate_w.at[rows_of(number), pl.ds((kind - 1) * share, share)]

    def cast(kinds):
        @pl.when(sends)
        def _():
            for kind in kinds:
                source_of(
                    kind, rank,
                    lambda src: pltpu.make_async_copy(
                        src, landing(kind, me), own_sem.at[kind]
                    ).start(),
                )

            def body(i):
                target = lax.rem(me + 1 + i, PLACES)
                for kind in kinds:
                    source_of(
                        kind, lax.rem(target, RANKS),
                        lambda src: copied(
                            src, landing(kind, me), w_send.at[kind, i], w_recv.at[kind, mine],
                            in_plane(target),
                        ).start(),
                    )

            loop(PLACES - 1, body)

    def swap(kind, number):
        block = (mod_w, gate_w, in_w)[kind].at[rows_of(2 * number + half)]
        return copied(block, block, xs_send.at[kind, number], xs_recv.at[kind, number], across)

    def take(kinds, swap_kinds):
        def body(i):
            number = lax.rem(lax.div(me + PLACES - half, 2) + RANKS - i, RANKS)
            source = 2 * number + half

            @pl.when(source != me)
            def _():
                for kind in kinds:
                    block = landing(kind, source)
                    copied(
                        block, block, w_send.at[kind, 0], w_recv.at[kind, number], across
                    ).wait_recv()

            @pl.when(source == me)
            def _():
                for kind in kinds:
                    block = landing(kind, me)
                    pltpu.make_async_copy(block, block, own_sem.at[kind]).wait()

            for kind in swap_kinds:
                swap(kind, number).start()

        loop(RANKS, body)

    def row_copy(which, target_group):
        src, dst = ((project_out, out_w.at[half, pl.ds(0, high)]), (down, down_w.at[half]))[which]
        return copied(
            src, dst, r_send.at[which, target_group], r_recv.at[which, 0],
            in_plane(target_group * RANKS + mine),
        )

    def row_own(which):
        src, dst = ((project_out, out_w.at[half, pl.ds(0, high)]), (down, down_w.at[half]))[which]
        return pltpu.make_async_copy(src, dst, own_sem.at[4 + which])

    def row_swap(which):
        block = (out_w.at[half, pl.ds(0, high)], down_w.at[half])[which]
        return copied(block, block, r_send.at[which, 2], r_recv.at[which, 1], across)

    cast((0,))
    cond_own[group] = condition[group]
    partner.wait()
    raw = cond_own[...].astype(F32)
    cond_all[rank] = mat(raw * sigma(raw)).astype(BF16)
    gather = Gather(place, cond_all, sems)
    gather.start()
    cast((3, 1, 2))
    for which in range(2):
        for target_group in range(2):
            target = target_group * RANKS + mine

            @pl.when(sends & (target != me))
            def _():
                row_copy(which, target_group).start()

            @pl.when(sends & (target == me))
            def _():
                row_own(which).start()

    take((0,), (0,))

    def across_in(kind):
        def body(number):
            swap(kind, number).wait_recv()

        loop(RANKS, body)

    across_in(0)

    def give(k, flip):
        core = 1 - place.core if flip else place.core
        return sent(
            stage.at[k, core], mods.at[rank], sems, 6 if flip else 4, k, place.device(k, flip)
        )

    def body(k):
        gather.arrive(k)
        part = product(mat(cond_all[place.rows(k)]), mod_w[...], (1, 0)).astype(BF16)
        stage[k] = part.reshape(stage.shape[1:])
        give(k, True).start()

        @pl.when(k == 0)
        def _():
            mods[rank] = stage[0, place.core]

        @pl.when(k > 0)
        def _():
            give(k, False).start()

    chips(body)
    take((3, 1, 2), (2, 1))
    owner = 2 * rank + half
    for which in range(2):

        @pl.when(owner != me)
        def _():
            row_copy(which, 0).wait_recv()

        @pl.when(owner == me)
        def _():
            row_own(which).wait()

        row_swap(which).start()
    gather.finish()
    for k in range(CHIPS):
        give(k, True).wait()
        if k:
            give(k, False).wait()
    across_in(1)
    across_in(2)
    for which in range(2):
        row_swap(which).wait()
        for target_group in range(2):

            @pl.when(sends & (target_group * RANKS + mine != me))
            def _():
                row_copy(which, target_group).wait_send()

    @pl.when(sends)
    def _():
        def drain(i):
            for kind in range(4):
                block = landing(kind, me)
                copied(block, block, w_send.at[kind, i], w_recv.at[kind, 0], across).wait_send()

        loop(PLACES - 1, drain)

    def swapped_out(number):
        for kind in range(3):
            swap(kind, number).wait_send()

    loop(RANKS, swapped_out)


def start(modulation, final_modulation, gate_up, in_cols, project_out, down, condition):
    high, width = project_out.shape
    share = gate_up.shape[1] // (2 * RANKS)
    tokens = condition.shape[0] * condition.shape[1]
    outs = [
        (RANKS, tokens, width), (RANKS, tokens, width), condition.shape, (width, width),
        (width, 2 * share), (width, in_cols.shape[2]), (2, 128, width), (2, *down.shape),
    ]
    dma = pltpu.SemaphoreType.DMA
    return pl.pallas_call(
        start_kernel,
        out_shape=tuple(jax.ShapeDtypeStruct(shape, BF16) for shape in outs),
        in_specs=[pl.BlockSpec(memory_space=pl.ANY)] * 6 + [pl.BlockSpec(memory_space=pltpu.VMEM)],
        out_specs=tuple(pl.BlockSpec(memory_space=pltpu.VMEM) for _ in outs),
        scratch_shapes=[
            pltpu.VMEM((CHIPS, 2, tokens, width), BF16),
            dma((8, CHIPS)),
            dma((4, PLACES)), dma((4, RANKS)), dma((3, RANKS)), dma((3, RANKS)),
            dma((2, 3)), dma((2, 2)), dma((6,)), dma((2,)),
        ],
        compiler_params=pltpu.CompilerParams(
            collective_id=2, has_side_effects=True, vmem_limit_bytes=60 << 20
        ),
        name="start_kernel",
    )(modulation, final_modulation, gate_up, in_cols, project_out, down, condition)


class Crossing:
    def __init__(self, grads, land, sems, kind, high, by_place=True):
        self.grads, self.land, self.sems, self.kind = grads, land, sems, kind
        self.half, self.high, self.by_place = lax.axis_index("x"), high, by_place

    def copy(self, number, order):
        if self.by_place:
            first = (2 * number + 1 - self.half) * self.high
            block, land = self.grads.at[pl.ds(pl.multiple_of(first, 8), self.high)], self.land.at[number]
        else:
            first = (1 - self.half) * (self.grads.shape[0] // 2)
            block, land = self.grads.at[pl.ds(pl.multiple_of(first, 8), self.high)], self.land
        return copied(
            block, land, self.sems.at[self.kind, 0, order], self.sems.at[self.kind, 1, order],
            {"x": 1 - self.half},
        )

    def start(self):
        if self.by_place:
            loop(RANKS, lambda i: self.copy(i, i).start())
        else:
            self.copy(0, 0).start()

    def wait(self):
        if self.by_place:
            loop(RANKS, lambda i: self.copy(i, i).wait())
        else:
            self.copy(0, 0).wait()


def finish_kernel(
    mod_grad, gate_grad, gate_land, in_grad, in_land, down_grad, down_land, out_grad, out_land, small,
    mod_out, gate_out, in_out, down_out, out_out, small_out,
    mod_land, mod_stage, gate_stage, in_stage, down_stage, out_stage,
    mod_in, gate_in, in_in, down_in, out_in, small_in, small_sum, small_land,
    cross, send, recv, r_send, r_recv, x_send, x_recv, s_send, s_recv, sx_sem,
):
    half, group, rank = lax.axis_index("x"), lax.axis_index("h"), rank_of()
    me = group * RANKS + rank
    mine = lax.div(me, 2)
    high = mod_land.shape[1]
    across = {"x": 1 - half}
    owns = lax.rem(me, 2) == half
    greet_plane(me, half)
    mods = Crossing(mod_grad, mod_land, cross, 0, high)
    loop(RANKS, lambda i: mods.copy(lax.rem(mine + i, RANKS), i).start())

    def small_copy(step):
        other = lax.rem(me + step, PLACES)
        return copied(
            small.at[other], small_in.at[me], s_send.at[0, step], s_recv.at[0, step], in_plane(other)
        )

    loop(PLACES - 1, lambda i: small_copy(i + 1).start())
    small_in[me] = small[me]

    def own_rows(ref, number):
        first = pl.multiple_of((2 * number + half) * high, 8)
        return ref[pl.ds(first, high)].astype(F32)

    def pieces(kind):
        return ((mod_stage, mod_in), (gate_stage, gate_in), (in_stage, in_in))[kind]

    def scatter(kind, number):
        stage, landing = pieces(kind)
        return copied(
            stage.at[number], landing.at[me], send.at[kind, number], recv.at[kind, me],
            in_plane(2 * number + half),
        )

    def push(kind, grads, land, number):
        stage, landing = pieces(kind)
        stage[number] = (own_rows(grads, number) + land[number].astype(F32)).astype(BF16)

        @pl.when(2 * number + half != me)
        def _():
            scatter(kind, number).start()

        @pl.when(2 * number + half == me)
        def _():
            landing[me] = stage[number]

    def early(i):
        number = lax.rem(mine + i, RANKS)
        push(1, gate_grad, gate_land, number)
        push(2, in_grad, in_land, number)

    loop(RANKS, early)
    owner = 2 * rank + half
    rows = (
        (down_stage, down_in, down_grad, down_land, down_out),
        (out_stage, out_in, out_grad, out_land, out_out),
    )

    def row_copy(which, source_group):
        stage, landing = rows[which][:2]
        return copied(
            stage, landing.at[group], r_send.at[which], r_recv.at[which, source_group], in_plane(owner)
        )

    for which, (stage, landing, grads, land, _) in enumerate(rows):
        first = pl.multiple_of(half * (grads.shape[0] // 2), 8)
        kept = grads[pl.ds(first, land.shape[0])].astype(F32)
        stage[...] = (kept + land[...].astype(F32)).astype(BF16)
        for source_group in range(2):

            @pl.when((owner != me) & (group == source_group))
            def _():
                row_copy(which, source_group).start()

        @pl.when(owner == me)
        def _():
            landing[group] = stage[...]

    def late(i):
        number = lax.rem(mine + i, RANKS)
        mods.copy(number, i).wait()
        push(0, mod_grad, mod_land, number)

    loop(RANKS, late)

    loop(PLACES - 1, lambda i: small_copy(i + 1).wait())
    small_sum[...] = jnp.sum(small_in[...], axis=0)
    pair = copied(small_sum, small_land, sx_sem.at[0], sx_sem.at[1], across)
    pair.start()
    pair.wait()
    small_out[me] = small_sum[...] + small_land[...]

    def spread(step):
        other = lax.rem(me + step, PLACES)
        return copied(
            small_out.at[me], small_out.at[me], s_send.at[1, step], s_recv.at[1, step], in_plane(other)
        )

    loop(PLACES - 1, lambda i: spread(i + 1).start())

    def final(kind, index):
        if kind == 2:
            block = in_out
        else:
            out, count = (mod_out, gate_out)[kind], (mod_stage, gate_stage)[kind].shape[2]
            block = out.at[:, pl.ds(index * count, count)]
        return copied(block, block, x_send.at[kind, index], x_recv.at[kind, index], across)

    def final_rows(which):
        out = rows[which][4]
        return copied(out, out, x_send.at[3, which], x_recv.at[3, which], across)

    @pl.when(owns)
    def _():
        def got(kind, source):
            @pl.when(source != me)
            def _():
                landing = pieces(kind)[1].at[source]
                copied(
                    landing, landing, send.at[kind, 0], recv.at[kind, source], across
                ).wait_recv()

        for index in range(RANKS):
            got(1, index)
            got(1, RANKS + index)
            count = gate_stage.shape[2]
            added = gate_in[index].astype(F32) + gate_in[RANKS + index].astype(F32)
            gate_out[:, index * count : (index + 1) * count] = added.astype(BF16)
            final(1, index).start()
        for index in range(RANKS):
            got(2, index)
            got(2, RANKS + index)
            added = in_in[index].astype(F32) + in_in[RANKS + index].astype(F32)
            in_out[index] = added.astype(BF16)
        final(2, 0).start()
        for which, (_, landing, _, _, out) in enumerate(rows):
            for source_group in range(2):

                @pl.when(source_group * RANKS + mine != me)
                def _():
                    row_copy(which, source_group).wait_recv()

            out[...] = (landing[0].astype(F32) + landing[1].astype(F32)).astype(BF16)
            final_rows(which).start()
        for index in range(RANKS):
            got(0, index)
            got(0, RANKS + index)
            count = mod_stage.shape[2]
            added = mod_in[index].astype(F32) + mod_in[RANKS + index].astype(F32)
            mod_out[:, index * count : (index + 1) * count] = added.astype(BF16)
            final(0, index).start()
        for kind in range(2):
            for index in range(RANKS):
                final(kind, index).wait_send()
        final(2, 0).wait_send()
        for which in range(2):
            final_rows(which).wait_send()

    @pl.when(jnp.logical_not(owns))
    def _():
        for kind in range(2):
            for index in range(RANKS):
                final(kind, index).wait_recv()
        final(2, 0).wait_recv()
        for which in range(2):
            final_rows(which).wait_recv()

    loop(PLACES - 1, lambda i: spread(i + 1).wait())

    def drain(number):
        @pl.when(2 * number + half != me)
        def _():
            for kind in range(3):
                scatter(kind, number).wait_send()

    loop(RANKS, drain)
    for which in range(2):

        @pl.when(owner != me)
        def _():
            row_copy(which, 0).wait_send()


def finish(mod_grad, gate_grad, gate_land, in_grad, in_land, down_grad, down_land, out_grad, out_land, small):
    operands = (
        mod_grad, gate_grad, gate_land, in_grad, in_land, down_grad, down_land, out_grad, out_land, small,
    )
    high, width = out_land.shape
    gates, ins, downs = gate_grad.shape[1], in_grad.shape[1], down_land.shape[0]
    outs = [
        ((high, RANKS * width), BF16), ((high, RANKS * gates), BF16), ((RANKS, high, ins), BF16),
        ((downs, width), BF16), ((high, width), BF16), (small.shape, F32),
    ]
    work = [
        (RANKS, high, width), (RANKS, high, width), (RANKS, high, gates), (RANKS, high, ins),
        (downs, width), (high, width),
        (PLACES, high, width), (PLACES, high, gates), (PLACES, high, ins),
        (2, downs, width), (2, high, width),
    ]
    dma = pltpu.SemaphoreType.DMA
    return pl.pallas_call(
        finish_kernel,
        out_shape=tuple(jax.ShapeDtypeStruct(shape, kind) for shape, kind in outs),
        in_specs=[pl.BlockSpec(memory_space=pltpu.VMEM)] * len(operands),
        out_specs=tuple(pl.BlockSpec(memory_space=pltpu.VMEM) for _ in outs),
        scratch_shapes=[pltpu.VMEM(shape, BF16) for shape in work]
        + [pltpu.VMEM(small.shape, F32), pltpu.VMEM(small.shape[1:], F32), pltpu.VMEM(small.shape[1:], F32)]
        + [
            dma((1, 2, RANKS)), dma((3, RANKS)), dma((3, PLACES)), dma((2,)), dma((2, 2)),
            dma((4, RANKS)), dma((4, RANKS)), dma((2, PLACES)), dma((2, PLACES)), dma((2,)),
        ],
        compiler_params=pltpu.CompilerParams(
            collective_id=3, has_side_effects=True, vmem_limit_bytes=60 << 20
        ),
        name="finish_kernel",
    )(*operands)


def selection(wide_count, head, lanes):
    narrow = -(-(wide_count // lanes * head) // 128) * 128
    row = lax.broadcasted_iota(jnp.int32, (wide_count, narrow), 0)
    col = lax.broadcasted_iota(jnp.int32, (wide_count, narrow), 1)
    within = lax.rem(row, lanes)
    hit = (lax.div(row, lanes) * head + within == col) & (within < head)
    return jnp.where(hit, 1.0, 0.0).astype(BF16)


def shifted(shard, axes, by):
    size = math.prod(lax.axis_size(a) for a in axes)
    return lax.ppermute(shard, axes, [(i, (i + by) % size) for i in range(size)])


def swapped(both, group):
    kept = jnp.where(group == 0, both[0], both[1])
    sent = jnp.where(group == 0, both[1], both[0])
    got = lax.ppermute(sent, "h", [(0, 1), (1, 0)])
    return jnp.stack([jnp.where(group == 0, kept, got), jnp.where(group == 0, got, kept)])


def unfold(tile):
    count, height, across, chans = tile.shape
    cut = tile.reshape(count, height // PATCH, PATCH, across // PATCH, PATCH, chans)
    return cut.transpose(0, 1, 3, 2, 4, 5).reshape(count, -1, PATCH * PATCH * chans)


def refold(flat, count, height, across, chans):
    cut = flat.reshape(count, height // PATCH, across // PATCH, PATCH, PATCH, chans)
    return cut.transpose(0, 1, 3, 2, 4, 5).reshape(count, height, across, chans)


def normed(rows):
    inverse = lax.rsqrt(jnp.mean(rows * rows, axis=-1, keepdims=True) + EPSILON)
    return rows * inverse, inverse


def modnorm_back(grad, norm, inverse, scale):
    through = grad * (1.0 + scale)
    return inverse * (through - norm * jnp.mean(through * norm, axis=-1, keepdims=True))


def dot(left, right, contract, precision=None):
    return lax.dot_general(
        left, right, ((contract[:1], contract[1:]), ((), ())),
        precision=precision, preferred_element_type=F32,
    )


def sigma(v):
    return jax.nn.sigmoid(v)


def shards(
    latent, noise, timesteps, condition, embed_weight, embed_bias, modulation, modulation_bias,
    project_in, project_out, gate_up, down_weight, final_modulation, final_offsets, final_weight,
    final_bias, cotangent,
):
    highest = lax.Precision.HIGHEST
    images, height, across, chans = latent.shape
    width = condition.shape[-1]
    head = width // HEADS
    own_heads = HEADS // RANKS
    share = own_heads * head
    factor = 1.0 / math.sqrt(head)
    feed = gate_up.shape[-1] // 2
    feed_share = feed // RANKS
    high = modulation.shape[0]
    group = lax.axis_index("h")
    half = lax.axis_index("x")
    rank = rank_of()

    lanes = 128
    narrow = -(-3 * share // 128) * 128
    in_cols = project_in.reshape(high, 3, RANKS, share).transpose(2, 0, 1, 3)
    in_cols = jnp.pad(in_cols.reshape(RANKS, high, -1), ((0, 0), (0, 0), (0, narrow - 3 * share)))
    mods, cond_all, cond_own, mod_weight, gate_weight, in_narrow, out_weight, down_share = start(
        modulation, final_modulation, gate_up, in_cols, project_out, down_weight,
        condition.reshape(images, -1, width),
    )
    out_weight = out_weight.reshape(-1, width)
    down_share = down_share.reshape(-1, width)

    times = (timesteps.astype(F32) / 1000.0)[:, None, None, None]
    noisy = (1.0 - times) * latent + times * noise
    tiles = jnp.concatenate([noisy, cotangent], 3)
    tiles = jnp.concatenate([shifted(tiles[:, -1:], ("h", "l"), 1), tiles[:, :-1]], 1)
    tiles = jnp.concatenate([shifted(tiles[:, :, -1:], ("gx",), 1), tiles[:, :, :-1]], 2)
    flat = jnp.concatenate([unfold(tiles[..., :chans]), unfold(tiles[..., chans:])], 2)
    flat = swapped(flat, group).reshape(-1, 2 * PATCH * PATCH * chans)
    patches, grad_rows = jnp.split(flat, 2, axis=1)
    cond = cond_own.reshape(-1, width).astype(F32)
    cond_sigma = sigma(cond)
    own_shape, all_shape = (cond.shape[0], width), (RANKS, cond.shape[0], width)
    tokens = RANKS * cond.shape[0]

    def every(columns, kind):
        return ((RANKS, cond.shape[0], columns), kind)

    embedded = dot(patches, embed_weight, (1, 0), highest) + embed_bias
    bias = jnp.concatenate([modulation_bias, final_offsets]).reshape(RANKS, 1, width)
    shift_a, scale_a, gate_a, shift_b, scale_b, gate_b, shift_f, scale_f = mods.astype(F32) + bias
    norm_a, inv_a = normed(embedded)
    attend_in = (norm_a * (1.0 + scale_a) + shift_a).astype(BF16)
    branch, attend_all, qkv, mixed, in_weight = segment(
        functools.partial(attend_kernel, factor, head), 5, (attend_in, in_narrow, out_weight),
        [(own_shape, F32), (all_shape, BF16), every(6 * lanes, BF16), every(2 * lanes, BF16),
         ((width, 6 * lanes), BF16)],
        [], own_shape,
    )
    h_one = embedded + gate_a * branch
    norm_b, inv_b = normed(h_one)
    ffn_in = (norm_b * (1.0 + scale_b) + shift_b).astype(BF16)
    ffn, ffn_all, gateup = segment(
        feed_kernel, 6, (ffn_in, gate_weight, down_share),
        [(own_shape, F32), (all_shape, BF16), every(2 * feed_share, F32)], [], own_shape,
    )
    h_two = h_one + gate_b * ffn
    norm_f, inv_f = normed(h_two)
    final_in = norm_f * (1.0 + scale_f) + shift_f
    rows_out = dot(final_in, final_weight, (1, 0), highest) + final_bias

    final_bias_grad = jnp.sum(grad_rows, axis=0)
    final_weight_grad = dot(grad_rows, final_in, (0, 0), highest)
    grad_final_in = dot(grad_rows, final_weight, (1, 1), highest)
    grad_h_two = modnorm_back(grad_final_in, norm_f, inv_f, scale_f)
    grad_shift_f, grad_scale_f = grad_final_in, grad_final_in * norm_f
    grad_gate_b = grad_h_two * ffn
    grad_ffn_in, gate_grad, down_grad = segment(
        feed_back_kernel, 7,
        ((grad_h_two * gate_b).astype(BF16), gate_weight, down_share, gateup, ffn_all),
        [(own_shape, F32), (gate_weight.shape, BF16), (down_share.shape, BF16)],
        [(all_shape, BF16), every(2 * feed_share, BF16), every(feed_share, BF16)], own_shape,
    )
    grad_h_one = grad_h_two + modnorm_back(grad_ffn_in, norm_b, inv_b, scale_b)
    grad_shift_b, grad_scale_b = grad_ffn_in, grad_ffn_in * norm_b
    grad_gate_a = grad_h_one * branch
    grad_attend, in_grad, out_grad, gate_land, down_land = segment(
        functools.partial(attend_back_kernel, factor, head), 8,
        ((grad_h_one * gate_a).astype(BF16), in_weight, out_weight, attend_all, qkv, mixed,
         gate_grad, down_grad),
        [(own_shape, F32), (in_narrow.shape, BF16), (out_weight.shape, BF16),
         ((RANKS, high, 2 * feed_share), BF16), ((feed_share // 2, width), BF16)],
        [(all_shape, BF16), every(2 * lanes, BF16), every(6 * lanes, BF16),
         ((2, tokens, lanes), F32), ((2, tokens, lanes), F32)], own_shape, True,
    )
    grad_embedded = grad_h_one + modnorm_back(grad_attend, norm_a, inv_a, scale_a)
    grad_shift_a, grad_scale_a = grad_attend, grad_attend * norm_a
    grad_mods = jnp.stack(
        [grad_shift_a, grad_scale_a, grad_gate_a, grad_shift_b, grad_scale_b, grad_gate_b,
         grad_shift_f, grad_scale_f]
    )
    grad_cond, mod_grad, in_land, out_land = segment(
        mod_back_kernel, 9, (grad_mods.astype(BF16), mod_weight, cond_all, in_grad, out_grad),
        [(own_shape, F32), (mod_weight.shape, BF16), ((RANKS, high, narrow), BF16),
         ((high, width), BF16)], [(all_shape, BF16)], own_shape, True,
    )
    grad_cond = grad_cond * cond_sigma * (1.0 + cond * (1.0 - cond_sigma))
    grad_cond = swapped(grad_cond.astype(BF16).reshape(images, -1, width), group)
    condition_grad = grad_cond.astype(F32).reshape(condition.shape)

    embed_weight_grad = dot(patches, grad_embedded, (0, 0), highest)
    grad_patches = dot(grad_embedded, embed_weight, (1, 1), highest)
    small = jnp.concatenate(
        [
            jnp.sum(grad_mods, axis=1),
            jnp.sum(grad_embedded, axis=0, keepdims=True),
            embed_weight_grad,
            final_weight_grad,
            jnp.pad(final_bias_grad, (0, width - final_bias_grad.shape[0]))[None],
        ],
        0,
    )
    count = small.size
    part = -(-count // (PLACES * 1024)) * 1024
    small = jnp.pad(small.reshape(-1), (0, PLACES * part - count)).reshape(PLACES, 8, -1)
    mods_out, gates_out, ins_out, down_out, out_out, small = finish(
        mod_grad, gate_grad, gate_land, in_grad, in_land, down_grad, down_land, out_grad, out_land, small
    )

    def images_sum(value):
        value = value.astype(F32)
        return lax.psum(value, "ih") if lax.axis_size("ih") > 1 else value

    small = images_sum(small).reshape(-1)[:count].reshape(-1, width)
    mod_bias_grad = small[:6].reshape(-1)
    offsets_grad = small[6:8].reshape(-1)
    embed_bias_grad = small[8]
    patch = PATCH * PATCH * chans
    embed_weight_grad = small[9 : 9 + patch]
    final_weight_grad = small[9 + patch : 9 + 2 * patch].T
    final_bias_grad = small[9 + 2 * patch, :patch]

    flat = jnp.concatenate([rows_out, grad_patches], 1).reshape(images, -1, 2 * patch)
    flat = swapped(flat, group)
    tiles = jnp.concatenate(
        [refold(flat[..., :patch], images, height, across, chans),
         refold(flat[..., patch:], images, height, across, chans)], 3)
    tiles = jnp.concatenate([tiles[:, 1:], shifted(tiles[:, :1], ("h", "l"), -1)], 1)
    tiles = jnp.concatenate([tiles[:, :, 1:], shifted(tiles[:, :, :1], ("gx",), -1)], 2)
    prediction = tiles[..., :chans]
    latent_grad = (1.0 - times) * tiles[..., chans:]

    mods_out, gate_up_grad = images_sum(mods_out), images_sum(gates_out)
    gate_up_grad = gate_up_grad.reshape(high, RANKS, 2, feed_share).transpose(0, 2, 1, 3)
    project_in_grad = images_sum(ins_out)[..., : 3 * share].reshape(RANKS, high, 3, share)
    project_in_grad = project_in_grad.transpose(1, 2, 0, 3).reshape(high, -1)
    return (
        prediction,
        latent_grad,
        condition_grad,
        embed_weight_grad,
        embed_bias_grad,
        mods_out[:, : 6 * width],
        mod_bias_grad,
        project_in_grad,
        images_sum(out_out),
        gate_up_grad.reshape(high, -1),
        images_sum(down_out),
        mods_out[:, 6 * width :],
        offsets_grad,
        final_weight_grad,
        final_bias_grad,
    )


def solution(mesh):
    pairs = mesh.shape["img"] // 2
    split = Mesh(
        mesh.devices.reshape(pairs, 2, 2, mesh.shape["gy"] // 2, mesh.shape["gx"]),
        ("ih", "x", "h", "l", "gx"),
    )
    img, gy, gx = ("ih", "x"), ("h", "l"), "gx"
    tiles = P(img, gy, gx, None)
    held = P(("h", "l", "gx"), None)
    in_specs = (
        tiles, tiles, P(img), tiles, P(), P(), held, P(), held, held, held, held, held, P(), P(), P(), tiles,
    )
    out_specs = (
        tiles, tiles, tiles, P(), P(), held, P(), held, held, held, held, held, P(), P(), P(),
    )
    return jax.shard_map(shards, mesh=split, in_specs=in_specs, out_specs=out_specs, check_vma=False)
```

time: 1710 us -> 538 us (0.31)
  waiting for transfers between devices: 1390 us -> 9.67 us
  Pallas kernels: 0 us -> 440 us
  matrix products: 151 us -> 4.7 us
  blocking collectives: 38.2 us -> 0 us
  local copies, waits for them, and re-layouts: 53.3 us -> 31.2 us
    reduce_scatter x6 -> x0, waiting for transfers between devices: 610 us -> none  [the longest x1 176 us: shards(): lax.psum_scatter(mod_full.astype(jnp.bfloat16), ('gy', 'gx'), scatter_dim...]
    all_gather x8 -> x0, waiting for transfers between devices: 494 us -> none  [the longest x1 112 us: shards(): lax.all_gather(modulation, ('gy', 'gx'), axis=0, tiled=True)]
    pallas_call x0 -> x7, Pallas kernels: none -> 440 us  [the longest x5 232 us: segment(): pl.pallas_call(kernel, out_shape=tuple((jax.ShapeDtypeStruct(shape, kind)...]
    dot_general x30 -> x6, matrix products: 151 us -> 4.7 us  [dot(): lax.dot_general(left, right, ((contract[:1], contract[1:]), ((), ())), pr...]
    unnamed x20 -> x0, waiting for transfers between devices: 134 us -> none
    psum x2 -> x0, waiting for transfers between devices: 133 us -> none  [the longest x1 119 us: shards(): lax.psum((embed_weight_grad, embed_bias_grad, modulation_bias_grad, final...]
    psum x1 -> x0, blocking collectives: 38.2 us -> none  [shards(): lax.psum((embed_weight_grad, embed_bias_grad, modulation_bias_grad, final...]
  transfers between devices with their start and end apart: 26 -> 7, of which waited for: 25 -> 3; matrix products, arithmetic and copies ran while one was open for 11% -> 6% of each run, Pallas kernels for 0% -> 20%
where the time goes in v1:
time: 538 us; the launch traced here: 537 us
  Pallas kernels  440 us (82%)
  other arithmetic  33.2 us (6%)
  local copies, waits for them, and re-layouts  31.2 us (6%)
  starting transfers between devices  16.7 us (3%)
  waiting for transfers between devices  9.67 us (2%)
    pallas_call x5, Pallas kernels, segment(): pl.pallas_call(kernel, out_shape=tuple((jax.ShapeDtypeStruct(shape, kind)...  232 us
    pallas_call x1, Pallas kernels, start(): pl.pallas_call(start_kernel, out_shape=tuple((jax.ShapeDtypeStruct(shape,...  110 us
    pallas_call x1, Pallas kernels, finish(): pl.pallas_call(finish_kernel, out_shape=tuple((jax.ShapeDtypeStruct(shape...  98.7 us
    ppermute x4, starting transfers between devices, shifted(): lax.ppermute(shard, axes, [(i, (i + by) % size) for i in range(size)])  14.2 us
  transfers between devices with their start and end apart: 7, of which 3 were waited for; matrix products, arithmetic and copies ran while one was open for 6% of the time, Pallas kernels for 20%

profile of v1, /device:TPU:1, one launch (start us, length us, event | category | flops | bytes accessed | tf_op | source)
XLA Modules:
  0.0 537.2 jit_solution(9821706039144384938)
XLA Ops:
  4.8 2.1 collective-permute-start
  7.7 2.4 collective-permute-done
  10.2 2.9 collective-permute-start.1
  13.2 2.4 reshape.194
  18.3 109.6 %start_kernel.1 = (bf16[8,128,1152]{2,1,0:T(8,128)(2,1)}, bf16[8,128,1152]{2,1,0:T(8,128)(2,1)}, bf16[2,64,1152]{2,1,0:T(8,128)(2,1)}, bf16[1152,1152]{1,0:T(8,1...) custom-call(bf16[72,6912]{1,0:T(8,128)(2,1)} %modulation.1, ...), custom_call_target="tpu_custom_call" | custom-call | tf_op jit(solution)/shard_map/start_kernel/pallas_call | solution.py:694
  129.5 4.2 convert_add_fusion
  134.6 2.1 fusion.12.own
  136.8 50.4 %attend_kernel.1 = (f32[128,1152]{1,0:T(8,128)}, bf16[8,128,1152]{2,1,0:T(8,128)(2,1)}, bf16[8,128,768]{2,1,0:T(8,128)(2,1)}, bf16[8,128,256]{2,1,0:T(8,128)(2,1)}, bf16[1152,768]{1,0:T(8,128)(2,1)}) custom-call(bf16[128,1152]{1,0:T(8,128)(2,1)} %fusion.12.own, bf16[1152,512]{1,0:T(8,128)(2,1)} %get-tuple-element.50.in_narrow, bf16[256,1152]{1,0:T(8,128)(2,1)} %bitcast.162), custom_call_target="tpu_custom_call" | custom-call | tf_op jit(solution)/shard_map/attend_kernel/pallas_call | solution.py:435
  188.7 2.1 fusion.9.own
  190.8 39.1 %feed_kernel.1 = (f32[128,1152]{1,0:T(8,128)}, bf16[8,128,1152]{2,1,0:T(8,128)(2,1)}, f32[8,128,768]{2,1,0:T(8,128)}) custom-call(bf16[128,1152]{1,0:T(8,128)(2,1)} %fusion.9.own, bf16[1152,768]{1,0:T(8,128)(2,1)} %get-tuple-element.53.gate_weight, bf16[384,1152]{1,0:T(8,128)(2,1)} %bitcast.159), custom_call_target="tpu_custom_call" | custom-call | tf_op jit(solution)/shard_map/feed_kernel/pallas_call | solution.py:435
  231.5 1.9 multiply_reduce_fusion.2
  233.4 2.4 multiply_convert_fusion.1
  235.8 39.1 %feed_back_kernel.1 = (f32[128,1152]{1,0:T(8,128)}, bf16[1152,768]{1,0:T(8,128)(2,1)}, bf16[384,1152]{1,0:T(8,128)(2,1)}) custom-call(bf16[128,1152]{1,0:T(8,128)(2,1)} %get-tuple-element.117.own, bf16[1152,768]{1,0:T(8,128)(2,1)} %get-tuple-element.53.gate_weight, bf16[384,1152]{1,0:T(8,128)(2,1)} %bitcast.160, f32[8,128,768]{2,1,0:T(8,128)} %get-tuple-element.56.gateup, ...), custom_call_target="tpu_custom_call" | custom-call | tf_op jit(solution)/shard_map/feed_back_kernel/pallas_call | solution.py:435
  276.4 2.6 multiply_convert_fusion
  279.0 46.4 %attend_back_kernel.1 = (f32[128,1152]{1,0:T(8,128)}, bf16[1152,512]{1,0:T(8,128)(2,1)}, bf16[256,1152]{1,0:T(8,128)(2,1)}, bf16[8,72,768]{2,1,0:T(8,128)(2,1)}, bf16[192,1152]{1,0:T(8,128)(2,1)}) custom-call(bf16[128,1152]{1,0:T(8,128)(2,1)} %get-tuple-element.115.own, bf16[1152,768]{1,0:T(8,128)(2,1)} %get-tuple-element.59.in_weight, ...), custom_call_target="tpu_custom_call" | custom-call | tf_op jit(solution)/shard_map/attend_back_kernel/pallas_call | solution.py:435
  335.2 57.3 %mod_back_kernel.1 = (f32[128,1152]{1,0:T(8,128)}, bf16[1152,1152]{1,0:T(8,128)(2,1)}, bf16[8,72,512]{2,1,0:T(8,128)(2,1)}, bf16[72,1152]{1,0:T(8,128)(2,1)}) custom-call(bf16[8,128,1152]{2,1,0:T(8,128)(2,1)} %get-tuple-element.125.own, bf16[1152,1152]{1,0:T(8,128)(2,1)} %get-tuple-element.66.weight, bf16[8,128,1152]{2,1,0:T(8,128)(2,1)} %get-tuple-element.67.cond_all, ...), custom_call_target="tpu_custom_call" | custom-call | tf_op jit(solution)/shard_map/mod_back_kernel/pallas_call | solution.py:435
  392.4 98.7 %finish_kernel.1 = (bf16[72,9216]{1,0:T(8,128)(2,1)}, bf16[72,6144]{1,0:T(8,128)(2,1)}, bf16[8,72,512]{2,1,0:T(8,128)(2,1)}, bf16[192,1152]{1,0:T(8,128)(2,1)}, ...) custom-call(bf16[1152,1152]{1,0:T(8,128)(2,1)} %get-tuple-element.72.mod_grad, ...), custom_call_target="tpu_custom_call" | custom-call | tf_op jit(solution)/shard_map/finish_kernel/pallas_call | solution.py:948
  491.1 2.3 slice_convert_fusion
  502.4 2.0 copy.64
  504.4 2.9 reshape.215
  514.1 2.4 collective-permute-start.6
  517.7 7.1 %collective-permute-start.4 = (f32[2,1,16,8]{3,2,1,0:T(8,128)S(1)}, f32[2,1,16,8]{3,2,1,0:T(8,128)S(1)}, u32[]{:S(2)}, u32[]{:S(2)}) collective-permute-start(f32[2,1,16,8]{3,2,1,0:T(8,128)S(1)} %pad_maximum_fusion.6), channel_id=1, source_target_pairs={{0,12},{4,0},{8,4},{12,8},{1,13},{5,1},{9,5},{13,9},{2,14},{6,2},{... | collective-permute-start | bytes 3080 | tf_op jit(solution)/shard_map/ppermute | solution.py:977
  526.2 2.0 collective-permute-start.5
  528.3 6.0 %collective-permute-done.5 = f32[2,16,1,8]{3,2,1,0:T(1,128)S(1)} collective-permute-done((f32[2,16,1,8]{3,2,1,0:T(1,128)S(1)}, f32[2,16,1,8]{3,2,1,0:T(1,128)S(1)}, u32[]{:S(2)}, u32[]{:S(2)}) %collective-permute-start.5) | collective-permute-done | bytes 1056 | tf_op jit(solution)/shard_map/ppermute | solution.py:977
  (138 shorter events, 45.5 us)
Async XLA Ops:
  0.6 133.2 %copy-start = (f32[16,1152]{1,0:T(8,128)S(1)}, f32[16,1152]{1,0:T(8,128)}, u32[]{:S(2)}) copy-start(f32[16,1152]{1,0:T(8,128)} %param.21) | copy-start | bytes 221188
  1.4 11.8 %copy-start.16 = (f32[2]{0:T(128)}, f32[2]{0:T(128)S(1)}, u32[]{:S(2)}) copy-start(f32[2]{0:T(128)S(1)} %get-tuple-element.140) | copy-start | bytes 28
  4.8 5.3 collective-permute-start
  10.2 117.7 %collective-permute-start.1 = (f32[2,16,1,8]{3,2,1,0:T(1,128)S(1)}, f32[2,16,1,8]{3,2,1,0:T(1,128)S(1)}, u32[]{:S(2)}, u32[]{:S(2)}) collective-permute-start(f32[2,16,1,8]{3,2,1,0:T(1,128)S(1)} %pad_maximum_fusion.9), channel_id=1, source_target_pairs={{0,1},{1,2},{2,3},{3,0},{4,5},{5,6},{6,7},{7,4},{8,9},{9,10},{10,1... | collective-permute-start | bytes 3080 | tf_op jit(solution)/shard_map/ppermute | solution.py:977
  128.0 5.8 %copy-start.15 = (f32[1152]{0:T(1024)S(1)}, f32[1152]{0:T(1024)}, u32[]{:S(2)}) copy-start(f32[1152]{0:T(1024)} %param.22) | copy-start | bytes 13828
  129.4 4.3 collective-permute-start.2
  187.2 44.3 %copy-start.11 = (f32[1152,16]{0,1:T(8,128)S(1)}, f32[1152,16]{0,1:T(8,128)}, u32[]{:S(2)}) copy-start(f32[1152,16]{0,1:T(8,128)} %param.31) | copy-start | bytes 221188
  325.4 5.7 %copy-start.3 = (f32[128,1152]{1,0:T(8,128)S(1)}, f32[128,1152]{1,0:T(8,128)}, u32[]{:S(2)}) copy-start(f32[128,1152]{1,0:T(8,128)} %get-tuple-element.65) | copy-start | bytes 1769476
  325.4 5.8 %copy-start.5 = (f32[128,1152]{1,0:T(8,128)S(1)}, f32[128,1152]{1,0:T(8,128)}, u32[]{:S(2)}) copy-start(f32[128,1152]{1,0:T(8,128)} %get-tuple-element.116) | copy-start | bytes 1769476
  325.4 5.8 %copy-start.7 = (f32[128,1152]{1,0:T(8,128)S(1)}, f32[128,1152]{1,0:T(8,128)}, u32[]{:S(2)}) copy-start(f32[128,1152]{1,0:T(8,128)} %get-tuple-element.52) | copy-start | bytes 1769476
  326.6 4.7 copy-start.2
  392.4 102.1 %copy-start.12 = (bf16[2,64,1152]{2,1,0:T(8,128)(2,1)S(1)}, bf16[2,64,1152]{2,1,0:T(8,128)(2,1)}, u32[]{:S(2)}) copy-start(bf16[2,64,1152]{2,1,0:T(8,128)(2,1)} %get-tuple-element.71) | copy-start | bytes 884740
  392.4 104.0 %copy-start.18 = (f32[16]{0:T(128)S(1)}, f32[16]{0:T(128)}, u32[]{:S(2)}) copy-start(f32[16]{0:T(128)} %param.32) | copy-start | bytes 196
  491.1 6.6 %copy-start.4 = (bf16[72,9216]{1,0:T(8,128)(2,1)S(1)}, bf16[72,9216]{1,0:T(8,128)(2,1)}, u32[]{:S(2)}) copy-start(bf16[72,9216]{1,0:T(8,128)(2,1)} %get-tuple-element.78) | copy-start | bytes 3981316
  497.1 4.7 copy-start.6
  497.2 19.2 %collective-permute-start.3 = (f32[64,32]{0,1:T(8,128)S(1)}, f32[64,32]{0,1:T(8,128)S(1)}, u32[]{:S(2)}, u32[]{:S(2)}) collective-permute-start(f32[64,32]{0,1:T(8,128)S(1)} %fusion.24), channel_id=1, source_target_pairs={{0,8},{8,0},{1,9},{9,1},{2,10},{10,2},{3,11},{11,3},{4,12},{12,4},... | collective-permute-start | bytes 24584 | tf_op jit(solution)/shard_map/ppermute | solution.py:983
  502.4 4.9 copy-start.9
  509.1 4.2 copy-start.13
  509.1 4.9 copy-start.14
  509.3 25.1 %copy-start.17 = (f32[2]{0:T(128)S(1)}, f32[2]{0:T(128)}, u32[]{:S(2)}) copy-start(f32[2]{0:T(128)} %copy-done.16) | copy-start | bytes 28
  509.3 27.9 %copy-start.1 = (f32[16,1152]{1,0:T(8,128)S(1)}, f32[16,1152]{1,0:T(8,128)}, u32[]{:S(2)}) copy-start(f32[16,1152]{1,0:T(8,128)} %param.21) | copy-start | bytes 221188
  514.1 22.2 %collective-permute-start.6 = (bf16[64,1152]{1,0:T(8,128)(2,1)S(1)}, bf16[64,1152]{1,0:T(8,128)(2,1)S(1)}, u32[]{:S(2)}, u32[]{:S(2)}) collective-permute-start(bf16[64,1152]{1,0:T(8,128)(2,1)S(1)} %copy-done.14), channel_id=1, source_target_pairs={{0,8},{8,0},{1,9},{9,1},{2,10},{10,2},{3,11},{11,3},{4,12},{12,4},... | collective-permute-start | bytes 442376 | tf_op jit(solution)/shard_map/ppermute | solution.py:983
  517.7 8.5 %collective-permute-start.4 = (f32[2,1,16,8]{3,2,1,0:T(8,128)S(1)}, f32[2,1,16,8]{3,2,1,0:T(8,128)S(1)}, u32[]{:S(2)}, u32[]{:S(2)}) collective-permute-start(f32[2,1,16,8]{3,2,1,0:T(8,128)S(1)} %pad_maximum_fusion.6), channel_id=1, source_target_pairs={{0,12},{4,0},{8,4},{12,8},{1,13},{5,1},{9,5},{13,9},{2,14},{6,2},{... | collective-permute-start | bytes 3080 | tf_op jit(solution)/shard_map/ppermute | solution.py:977
  526.2 8.1 %collective-permute-start.5 = (f32[2,16,1,8]{3,2,1,0:T(1,128)S(1)}, f32[2,16,1,8]{3,2,1,0:T(1,128)S(1)}, u32[]{:S(2)}, u32[]{:S(2)}) collective-permute-start(f32[2,16,1,8]{3,2,1,0:T(1,128)S(1)} %pad_maximum_fusion.5), channel_id=1, source_target_pairs={{0,3},{1,0},{2,1},{3,2},{4,7},{5,4},{6,5},{7,6},{8,11},{9,8},{10,9... | collective-permute-start | bytes 3080 | tf_op jit(solution)/shard_map/ppermute | solution.py:977
  (2 other events, 5.1 us)
